TPU v7x, 256 devices: a whole 4x4x8 slice. The times are simulated.
256 devices in a mesh: dp: 8 (over y, core), seq: 32 (over z, x).
Axes of the slice: x: 4, y: 4, z: 8, core: 2. Of those that a mesh axis runs over, the one named last changes fastest.
Arguments:
- query_rows: bfloat16 [8, 8192, 1536], P('dp', 'seq'), may hold values from -36 to 36, as said below
- key_rows: bfloat16 [8, 8192, 1536], P('dp', 'seq'), may hold values from -6 to 6
- value_rows: bfloat16 [8, 8192, 1536], P('dp', 'seq'), may hold values from -6 to 6
- norm_gain: float32 [1536], replicated, may hold values from 0.1 to 1.9
- grad_output: bfloat16 [8, 8192, 1536], P('dp', 'seq'), may hold values from -6 to 6
Outputs:
- attended: bfloat16 [8, 8192, 1536], P('dp', 'seq')
- grad_query: bfloat16 [8, 8192, 1536], P('dp', 'seq')
- grad_key: bfloat16 [8, 8192, 1536], P('dp', 'seq')
- grad_value: bfloat16 [8, 8192, 1536], P('dp', 'seq')
- grad_gain: float32 [1536], replicated
Inputs may be any that keep to these rules, and one draw needn't show every extreme that they name: `query_rows`: query features.
All inputs are finite; a program needn't handle non-finite values.
Results may differ from a plain program's by a relative error of at most 0.0057.
Values sent between devices are 32-bit elements; how exact they have to be, the bound alone decides.
A program may use at most 128 MiB of HBM per device.

v0:
```python
import jax
import jax.numpy as jnp
from jax import lax
from jax.sharding import PartitionSpec as P

HEADS = 12
HEAD_DIM = 128
BLOCK = 256
GAIN_PAD = 16384
norm_eps = 1e-05


def carried_in(value, axis, backward):
    count = lax.axis_size(axis)
    lanes = value.shape[-1]
    rows = value.reshape(count, -1, lanes)
    parts = lax.all_to_all(rows, axis, 0, 0)
    row = lax.broadcasted_iota(jnp.int32, (count, count), 0)
    col = lax.broadcasted_iota(jnp.int32, (count, count), 1)
    strict = row < col if backward else row > col
    shifted = jnp.einsum(
        "ij,jkl->ikl",
        strict.astype(jnp.float32),
        parts,
        precision=lax.Precision.HIGHEST,
        preferred_element_type=jnp.float32,
    )
    back = lax.all_to_all(shifted, axis, 0, 0)
    return back.reshape(value.shape)


def lower_mask(length):
    row_index = lax.broadcasted_iota(jnp.int32, (length, length), 0)
    col_index = lax.broadcasted_iota(jnp.int32, (length, length), 1)
    return row_index >= col_index


def local(query_rows, key_rows, value_rows, norm_gain, grad_output):
    tokens = query_rows.shape[1]
    features = query_rows.shape[2]
    blocks = tokens // BLOCK
    block_shape = (blocks, BLOCK, HEADS, HEAD_DIM)
    queries = query_rows.reshape(block_shape)
    key_blocks = key_rows.reshape(block_shape)
    value_blocks = value_rows.reshape(block_shape)
    causal = lower_mask(BLOCK)
    local_states = jnp.einsum(
        "nchd,nche->nhde", key_blocks, value_blocks, preferred_element_type=jnp.float32
    )
    device_total = jnp.sum(local_states, axis=0)
    carried = carried_in(device_total, "seq", False)
    running = jnp.cumsum(local_states, axis=0)
    before = jnp.concatenate([local_states[:1] * 0.0, running[:-1]], axis=0)
    states = (carried[None] + before).astype(jnp.bfloat16)
    scores = jnp.einsum("nchd,nthd->nhct", queries, key_blocks, preferred_element_type=jnp.float32)
    weights = jnp.where(causal, scores, 0.0).astype(jnp.bfloat16)
    combined = jnp.einsum("nchd,nhde->nche", queries, states, preferred_element_type=jnp.float32)
    combined = combined + jnp.einsum(
        "nhct,nthe->nche", weights, value_blocks, preferred_element_type=jnp.float32
    )
    combined = combined.reshape(1, tokens, features)
    inverse = lax.rsqrt(jnp.mean(combined * combined, axis=-1, keepdims=True) + norm_eps)
    normed = combined * inverse
    attended = (normed * norm_gain).astype(jnp.bfloat16)
    upstream = grad_output.astype(jnp.float32)
    gain_terms = jnp.sum(upstream * normed, axis=(0, 1))
    grad_normed = upstream * norm_gain
    grad_combined = inverse * (
        grad_normed - normed * jnp.mean(grad_normed * normed, axis=-1, keepdims=True)
    )
    grad_blocks = grad_combined.astype(jnp.bfloat16).reshape(block_shape)
    query_parts = jnp.einsum(
        "nchd,nche->nhde", queries, grad_blocks, preferred_element_type=jnp.float32
    )
    suffix = carried_in(jnp.sum(query_parts, axis=0), "seq", True)
    grad_gain = lax.psum(jnp.pad(gain_terms, (0, GAIN_PAD - features)), ("dp", "seq"))[:features]
    from_end = lax.cumsum(query_parts, axis=0, reverse=True)
    behind = jnp.concatenate([from_end[1:], query_parts[-1:] * 0.0], axis=0)
    suffix_states = (suffix[None] + behind).astype(jnp.bfloat16)
    grad_scores = jnp.einsum(
        "nche,nthe->nhct", grad_blocks, value_blocks, preferred_element_type=jnp.float32
    )
    grad_weights = jnp.where(causal, grad_scores, 0.0).astype(jnp.bfloat16)
    grad_query = jnp.einsum(
        "nche,nhde->nchd", grad_blocks, states, preferred_element_type=jnp.float32
    )
    grad_query = grad_query + jnp.einsum(
        "nhct,nthd->nchd", grad_weights, key_blocks, preferred_element_type=jnp.float32
    )
    grad_key = jnp.einsum(
        "nche,nhde->nchd", value_blocks, suffix_states, preferred_element_type=jnp.float32
    )
    grad_key = grad_key + jnp.einsum(
        "nhct,nchd->nthd", grad_weights, queries, preferred_element_type=jnp.float32
    )
    grad_value = jnp.einsum(
        "nchd,nhde->nche", key_blocks, suffix_states, preferred_element_type=jnp.float32
    )
    grad_value = grad_value + jnp.einsum(
        "nhct,nche->nthe", weights, grad_blocks, preferred_element_type=jnp.float32
    )
    out_shape = (1, tokens, features)
    return (
        attended,
        grad_query.reshape(out_shape).astype(jnp.bfloat16),
        grad_key.reshape(out_shape).astype(jnp.bfloat16),
        grad_value.reshape(out_shape).astype(jnp.bfloat16),
        grad_gain,
    )


def solution(mesh):
    placed = (
        P("dp", "seq", None),
        P("dp", "seq", None),
        P("dp", "seq", None),
        P(),
        P("dp", "seq", None),
    )
    return jax.shard_map(
        local,
        mesh=mesh,
        in_specs=placed,
        out_specs=(
            P("dp", "seq", None),
            P("dp", "seq", None),
            P("dp", "seq", None),
            P("dp", "seq", None),
            P(),
        ),
        check_vma=False,
    )
```

profile of v0, /device:TPU:1, one launch (start us, length us, event | category | flops | bytes accessed | tf_op | source)
XLA Modules:
  0.0 351.6 jit_solution(11559505907553414886)
XLA Ops:
  7.2 1.5 copy.60
  8.7 0.3 copy.61
  8.9 0.4 fusion.19
  9.3 0.0 copy-start.4
  9.3 32.7 %all_to_all.20 = f32[32,48,128]{2,1,0:T(8,128)S(1)} all-to-all(f32[32,48,128]{2,1,0:T(8,128)S(1)} %bitcast.104), channel_id=1, replica_groups=mesh['dp'=8,'seq'=32] {'seq'}, dimensions={0} | all-to-all | bytes 1572864 | tf_op jit(solution)/shard_map/all_to_all | solution.py:17
  42.0 0.8 fusion.13
  42.8 1.3 copy.64
  44.2 6.0 %all-to-all-start.1 = ((f32[32,48,128]{2,1,0:T(8,128)}), f32[32,48,128]{2,1,0:T(8,128)}, u32[]{:S(2)}, u32[]{:S(2)}) async-start(f32[32,48,128]{2,1,0:T(8,128)} %copy.64), calls=%async_computation.1 | async-start | bytes 1572864 | tf_op jit(solution)/shard_map/all_to_all | solution.py:28
  50.2 0.3 copy.70
  50.5 0.0 copy-start.2
  50.5 1.7 copy.65
  52.2 0.0 copy-start.11
  52.3 0.6 select_convert_fusion.1
  52.9 1.2 copy-done
  54.1 1.8 fusion.20
  55.9 14.1 %all-to-all-done.1 = f32[32,48,128]{2,1,0:T(8,128)} async-done(((f32[32,48,128]{2,1,0:T(8,128)}), f32[32,48,128]{2,1,0:T(8,128)}, u32[]{:S(2)}, u32[]{:S(2)}) %all-to-all-start.1) | async-done | bytes 786464 | tf_op jit(solution)/shard_map/all_to_all | solution.py:28
  70.0 1.6 add_convert_fusion.1
  71.6 0.3 copy-done.7
  71.9 0.4 fusion.8
  72.3 0.2 copy-done.12
  72.6 0.7 fusion.5
  73.3 2.5 fusion.4
  75.8 1.3 fusion.22
  77.1 6.8 %all-to-all-start.2 = ((f32[32,48,128]{2,1,0:T(8,128)}), f32[32,48,128]{2,1,0:T(8,128)}, u32[]{:S(2)}, u32[]{:S(2)}) async-start(f32[32,48,128]{2,1,0:T(8,128)} %bitcast.103), calls=%async_computation.2 | async-start | bytes 1572864 | tf_op jit(solution)/shard_map/all_to_all | solution.py:17
  83.9 0.0 all-reduce.3.cloned.1.call-start
  83.9 0.6 pad.4
  84.6 0.1 all-reduce.3.cloned.1.call-update
  84.6 19.0 %all-to-all-done.2 = f32[32,48,128]{2,1,0:T(8,128)} async-done(((f32[32,48,128]{2,1,0:T(8,128)}), f32[32,48,128]{2,1,0:T(8,128)}, u32[]{:S(2)}, u32[]{:S(2)}) %all-to-all-start.2) | async-done | bytes 786464 | tf_op jit(solution)/shard_map/all_to_all | solution.py:17
  103.6 1.9 fusion.11
  105.5 1.4 copy.76
  106.9 6.9 %all-to-all-start.3 = ((f32[32,48,128]{2,1,0:T(8,128)}), f32[32,48,128]{2,1,0:T(8,128)}, u32[]{:S(2)}, u32[]{:S(2)}) async-start(f32[32,48,128]{2,1,0:T(8,128)} %copy.76), calls=%async_computation.3 | async-start | bytes 1572864 | tf_op jit(solution)/shard_map/all_to_all | solution.py:28
  113.8 1.6 select_convert_fusion
  115.4 1.5 fusion.23
  117.0 1.6 fusion.24
  118.5 0.6 fusion.21
  119.2 1.2 fusion.7
  120.4 2.4 copy.80
  122.8 1.2 copy.81
  124.0 214.2 %all-reduce.3.cloned.1.call-done = f32[16384]{0:T(1024)} async-done(((f32[16384]{0:T(1024)}), f32[16384]{0:T(1024)}) %all-reduce.3.cloned.1.call-update) | async-done | bytes 65552 | tf_op jit(solution)/shard_map/psum | solution.py:76
  338.1 1.3 slice.4
  339.4 0.0 all-to-all-done.3
  339.5 1.4 fusion.10
  340.8 0.3 copy-done.6
  341.1 0.4 add_convert_fusion
  341.5 1.2 copy.83
  342.7 0.5 copy-done.5
  343.2 0.4 fusion.6
  343.6 1.2 copy.82
  (21 shorter events, 0.1 us)
Async XLA Ops:
  7.2 1.5 copy-start.9
  9.3 33.5 %copy-start.4 = (f32[12,128,128]{2,1,0:T(8,128)}, f32[12,128,128]{2,1,0:T(8,128)S(1)}, u32[]{:S(2)}) copy-start(f32[12,128,128]{2,1,0:T(8,128)S(1)} %fusion.19) | copy-start | bytes 2359300
  44.2 6.0 %copy-start.10 = (bf16[1,256,1536]{2,1,0:T(8,128)(2,1)S(1)}, bf16[1,256,1536]{2,1,0:T(8,128)(2,1)}, u32[]{:S(2)}) copy-start(bf16[1,256,1536]{2,1,0:T(8,128)(2,1)} %param.9) | copy-start | bytes 2359300
  44.2 25.8 %all-to-all-start.1 = ((f32[32,48,128]{2,1,0:T(8,128)}), f32[32,48,128]{2,1,0:T(8,128)}, u32[]{:S(2)}, u32[]{:S(2)}) async-start(f32[32,48,128]{2,1,0:T(8,128)} %copy.64), calls=%async_computation.1 | async-start | bytes 1572864 | tf_op jit(solution)/shard_map/all_to_all | solution.py:28
  50.5 21.8 %copy-start.2 = (bf16[1,256,1536]{1,2,0:T(8,128)(2,1)}, bf16[1,256,1536]{1,2,0:T(8,128)(2,1)S(1)}, u32[]{:S(2)}) copy-start(bf16[1,256,1536]{1,2,0:T(8,128)(2,1)S(1)} %copy.70) | copy-start | bytes 2359300
  52.2 0.7 copy-start.11
  52.9 1.2 copy-start
  70.0 1.9 copy-start.7
  71.9 0.7 copy-start.12
  77.1 26.5 %all-to-all-start.2 = ((f32[32,48,128]{2,1,0:T(8,128)}), f32[32,48,128]{2,1,0:T(8,128)}, u32[]{:S(2)}, u32[]{:S(2)}) async-start(f32[32,48,128]{2,1,0:T(8,128)} %bitcast.103), calls=%async_computation.2 | async-start | bytes 1572864 | tf_op jit(solution)/shard_map/all_to_all | solution.py:17
  83.9 254.3 %all-reduce.3.cloned.1.call-start = ((), (), s32[]{:S(2)}) async-start(), calls=%async_computation.4 | async-start | bytes 131072 | tf_op jit(solution)/shard_map/psum | solution.py:76
  106.9 232.6 %all-to-all-start.3 = ((f32[32,48,128]{2,1,0:T(8,128)}), f32[32,48,128]{2,1,0:T(8,128)}, u32[]{:S(2)}, u32[]{:S(2)}) async-start(f32[32,48,128]{2,1,0:T(8,128)} %copy.76), calls=%async_computation.3 | async-start | bytes 1572864 | tf_op jit(solution)/shard_map/all_to_all | solution.py:28
  113.8 1.6 copy-start.1
  120.4 2.4 copy-start.8
  120.4 219.0 %copy-start.3 = (f32[12,128,128]{1,2,0:T(8,128)S(1)}, f32[12,128,128]{1,2,0:T(8,128)}, u32[]{:S(2)}) copy-start(f32[12,128,128]{1,2,0:T(8,128)} %fusion.22) | copy-start | bytes 2359300
  339.4 1.6 copy-start.6
  341.5 1.7 copy-start.5
Sparse Core Ops, SparseCore 0:
  90.2 247.9 all-reduce.2
where the time goes:
time: 352 us
  waiting for transfers between devices  247 us (70%)
  blocking collectives  32.7 us (9%)
  starting transfers between devices  19.8 us (6%)
  local copies, waits for them, and re-layouts  16.7 us (5%)
  matrix products  14.5 us (4%)
  between operations  14.3 us (4%)
  other arithmetic  6.2 us (2%)
    psum x1, waiting for transfers between devices, local(): lax.psum(jnp.pad(gain_terms, (0, GAIN_PAD - features)), ('dp', 'seq'))  214 us
    all_to_all x1, blocking collectives, carried_in(): parts = lax.all_to_all(rows, axis, 0, 0)  32.7 us
    all_to_all x1, waiting for transfers between devices, carried_in(): parts = lax.all_to_all(rows, axis, 0, 0)  19 us
    all_to_all x2, waiting for transfers between devices, carried_in(): back = lax.all_to_all(shifted, axis, 0, 0)  14.1 us
    all_to_all x2, starting transfers between devices, carried_in(): back = lax.all_to_all(shifted, axis, 0, 0)  13 us
    unnamed x34, local copies, waits for them, and re-layouts  12.1 us
  transfers between devices with their start and end apart: 4, of which 3 were waited for; matrix products, arithmetic and copies ran while one was open for 6% of the time, Pallas kernels for 0%

commit v1 on v0

--- a/solution.py
+++ b/solution.py
@@ -73,7 +73,9 @@
         "nchd,nche->nhde", queries, grad_blocks, preferred_element_type=jnp.float32
     )
     suffix = carried_in(jnp.sum(query_parts, axis=0), "seq", True)
-    grad_gain = lax.psum(jnp.pad(gain_terms, (0, GAIN_PAD - features)), ("dp", "seq"))[:features]
+    grad_gain = jnp.sum(
+        lax.all_gather(jnp.pad(gain_terms, (0, GAIN_PAD - features)), ("dp", "seq")), axis=0
+    )[:features]
     from_end = lax.cumsum(query_parts, axis=0, reverse=True)
     behind = jnp.concatenate([from_end[1:], query_parts[-1:] * 0.0], axis=0)
     suffix_states = (suffix[None] + behind).astype(jnp.bfloat16)

time: 352 us -> 236 us (0.67)
  waiting for transfers between devices: 247 us -> 84 us
  blocking collectives: 32.7 us -> 59.7 us
  local copies, waits for them, and re-layouts: 16.7 us -> 36.5 us
  other arithmetic: 6.2 us -> 13.3 us
  starting transfers between devices: 19.8 us -> 12.8 us
    psum x1 -> x0, waiting for transfers between devices: 214 us -> none  [local(): lax.psum(jnp.pad(gain_terms, (0, GAIN_PAD - features)), ('dp', 'seq'))]
    all_gather x0 -> x1, waiting for transfers between devices: none -> 62.7 us  [local(): lax.all_gather(jnp.pad(gain_terms, (0, GAIN_PAD - features)), ('dp', 'seq'))]
    all_to_all x1 -> x2, blocking collectives: 32.7 us -> 59.7 us  [carried_in(): parts = lax.all_to_all(rows, axis, 0, 0)]
    all_to_all x1 -> x0, waiting for transfers between devices: 19 us -> none  [carried_in(): parts = lax.all_to_all(rows, axis, 0, 0)]
    all_gather x0 -> x1, local copies, waits for them, and re-layouts: none -> 18.2 us  [local(): lax.all_gather(jnp.pad(gain_terms, (0, GAIN_PAD - features)), ('dp', 'seq'))]
    all_to_all x2, waiting for transfers between devices: 14.1 us -> 21.3 us  [carried_in(): back = lax.all_to_all(shifted, axis, 0, 0)]
    all_to_all x1 -> x0, starting transfers between devices: 6.81 us -> none  [carried_in(): parts = lax.all_to_all(rows, axis, 0, 0)]
    reduce_sum x0 -> x1, other arithmetic: none -> 6.6 us  [local(): jnp.sum(lax.all_gather(jnp.pad(gain_terms, (0, GAIN_PAD - features)), ('d...]
  transfers between devices with their start and end apart: 4 -> 3, of which waited for: 3 -> 3; matrix products, arithmetic and copies ran while one was open for 6% -> 11% of each run, Pallas kernels for 0% -> 0%
where the time goes in v1:
time: 236 us; the launch traced here: 235 us
  waiting for transfers between devices  84 us (36%)
  blocking collectives  59.7 us (25%)
  local copies, waits for them, and re-layouts  36.5 us (15%)
  between operations  14.3 us (6%)
  matrix products  13.9 us (6%)
  other arithmetic  13.3 us (6%)
  starting transfers between devices  12.8 us (5%)
    all_gather x1, waiting for transfers between devices, local(): lax.all_gather(jnp.pad(gain_terms, (0, GAIN_PAD - features)), ('dp', 'seq'))  62.7 us
    all_to_all x2, blocking collectives, carried_in(): parts = lax.all_to_all(rows, axis, 0, 0)  59.7 us
    all_to_all x2, waiting for transfers between devices, carried_in(): back = lax.all_to_all(shifted, axis, 0, 0)  21.3 us
    all_gather x1, local copies, waits for them, and re-layouts, local(): lax.all_gather(jnp.pad(gain_terms, (0, GAIN_PAD - features)), ('dp', 'seq'))  18.2 us
    unnamed x38, local copies, waits for them, and re-layouts  14.4 us
    all_to_all x2, starting transfers between devices, carried_in(): back = lax.all_to_all(shifted, axis, 0, 0)  12.8 us
    reduce_sum x1, other arithmetic, local(): jnp.sum(lax.all_gather(jnp.pad(gain_terms, (0, GAIN_PAD - features)), ('d...  6.6 us
  transfers between devices with their start and end apart: 3, of which 3 were waited for; matrix products, arithmetic and copies ran while one was open for 11% of the time, Pallas kernels for 0%

profile of v1, /device:TPU:1, one launch (start us, length us, event | category | flops | bytes accessed | tf_op | source)
XLA Modules:
  0.0 234.5 jit_solution(4130343314908722574)
XLA Ops:
  7.2 1.5 copy.84
  8.7 0.3 copy.85
  8.9 0.4 fusion.19
  9.3 32.7 %all_to_all.20 = f32[32,48,128]{2,1,0:T(8,128)S(1)} all-to-all(f32[32,48,128]{2,1,0:T(8,128)S(1)} %bitcast.104), channel_id=1, replica_groups=mesh['dp'=8,'seq'=32] {'seq'}, dimensions={0} | all-to-all | bytes 1572864 | tf_op jit(solution)/shard_map/all_to_all | solution.py:17
  42.0 0.8 fusion.13
  42.8 1.3 copy.88
  44.2 5.9 %all-to-all-start.1 = ((f32[32,48,128]{2,1,0:T(8,128)}), f32[32,48,128]{2,1,0:T(8,128)}, u32[]{:S(2)}, u32[]{:S(2)}) async-start(f32[32,48,128]{2,1,0:T(8,128)} %copy.88), calls=%async_computation.1 | async-start | bytes 1572864 | tf_op jit(solution)/shard_map/all_to_all | solution.py:28
  50.1 0.0 all-gather.3.cloned.1.call-start
  50.2 0.3 copy.89
  50.4 1.4 copy.94
  51.9 0.6 select_convert_fusion.1
  52.5 0.1 copy-done.13
  52.7 1.2 copy-done.1
  53.8 1.8 fusion.20
  55.6 14.2 %all-to-all-done.1 = f32[32,48,128]{2,1,0:T(8,128)} async-done(((f32[32,48,128]{2,1,0:T(8,128)}), f32[32,48,128]{2,1,0:T(8,128)}, u32[]{:S(2)}, u32[]{:S(2)}) %all-to-all-start.1) | async-done | bytes 786464 | tf_op jit(solution)/shard_map/all_to_all | solution.py:28
  69.9 1.6 add_convert_fusion.1
  71.5 0.3 copy-done.10
  71.7 0.4 fusion.8
  72.2 1.1 copy-done
  73.3 0.7 fusion.5
  74.1 0.6 pad.4
  74.7 0.0 all-gather.3.cloned.1.call-update
  74.7 3.0 %fusion.4 = (bf16[1,256,1536]{1,2,0:T(8,128)(2,1)S(1)}, bf16[1,256,1536]{1,2,0:T(8,128)(2,1)}) fusion(bf16[1,256,1536]{1,2,0:T(8,128)(2,1)} %copy-done.4, f32[12,128,256]{2,1,0:T(8,128)} %copy-done, f32[256]{0:T(256)S(1)} %broadcast_multiply_fusion, f32[1536]{0:T(1024)S(1)} %copy-done.14, f32[256]{0:T(256)S(1)} %add_rsqrt_fusion), kind=kLoop, calls=%fused_computation.8 | loop fusion | flops 3538944 | bytes 3940352 | tf_op jit(solution)/shard_map/convert_element_type | solution.py:71
  77.7 0.4 fusion.22
  78.1 27.0 %all_to_all.21 = f32[32,48,128]{2,1,0:T(8,128)S(1)} all-to-all(f32[32,48,128]{2,1,0:T(8,128)S(1)} %bitcast.103), channel_id=1, replica_groups=mesh['dp'=8,'seq'=32] {'seq'}, dimensions={0} | all-to-all | bytes 1572864 | tf_op jit(solution)/shard_map/all_to_all | solution.py:17
  105.1 0.8 fusion.11
  105.9 1.4 copy.100
  107.2 6.9 %all-to-all-start.3 = ((f32[32,48,128]{2,1,0:T(8,128)}), f32[32,48,128]{2,1,0:T(8,128)}, u32[]{:S(2)}, u32[]{:S(2)}) async-start(f32[32,48,128]{2,1,0:T(8,128)} %copy.100), calls=%async_computation.3 | async-start | bytes 1572864 | tf_op jit(solution)/shard_map/all_to_all | solution.py:28
  114.1 1.5 select_convert_fusion
  115.6 0.6 fusion.21
  116.3 0.5 copy-done.2
  116.8 1.2 fusion.7
  118.0 2.3 copy.105
  120.3 2.3 copy.104
  122.6 3.1 %fusion.23 = f32[12,128,256]{2,1,0:T(8,128)} fusion(bf16[256,12,128]{0,2,1:T(8,128)(2,1)S(1)} %bitcast.102, bf16[12,256,256]{2,1,0:T(8,128)(2,1)} %copy-done.1), kind=kOutput, calls=%fused_computation.39 | convolution fusion | flops 201326592 | bytes 3932160 | tf_op jit(solution)/shard_map/nhct,nche->nthe/dot_general | solution.py:101
  125.6 1.6 fusion.24
  127.2 7.1 %all-to-all-done.3 = f32[32,48,128]{2,1,0:T(8,128)} async-done(((f32[32,48,128]{2,1,0:T(8,128)}), f32[32,48,128]{2,1,0:T(8,128)}, u32[]{:S(2)}, u32[]{:S(2)}) %all-to-all-start.3) | async-done | bytes 786464 | tf_op jit(solution)/shard_map/all_to_all | solution.py:28
  134.3 1.3 fusion.10
  135.6 0.3 copy-done.9
  135.9 0.4 add_convert_fusion
  136.3 1.2 copy.107
  137.5 0.5 copy-done.8
  138.0 0.4 fusion.6
  138.4 1.2 copy.106
  139.5 62.7 %all-gather.3.cloned.1.call-done = f32[4194304]{0:T(1024)} async-done(((f32[16384]{0:T(1024)}), f32[4194304]{0:T(1024)}) %all-gather.3.cloned.1.call-update) | async-done | bytes 16777232 | tf_op jit(solution)/shard_map/all_gather | solution.py:77
  202.3 18.2 %reshape.328 = f32[256,16384]{1,0:T(8,128)} reshape(f32[4194304]{0:T(1024)} %all-gather.3.cloned.1.call-done) | data formatting | bytes 33554432 | tf_op jit(solution)/shard_map/all_gather | solution.py:77
  220.5 6.6 %reduce_sum.41 = f32[16384]{0:T(1024)S(1)} reduce(f32[256,16384]{1,0:T(8,128)} %reshape.328, f32[]{:T(128)} %constant.3.clone.1), dimensions={0}, to_apply=%region_3.4 | reduce | flops 4177920 | bytes 16842756 | tf_op jit(solution)/shard_map/reduce_sum | solution.py:76
  227.1 0.6 slice.4
  (26 shorter events, 0.1 us)
Async XLA Ops:
  7.2 1.5 copy-start.11
  9.3 33.5 %copy-start.7 = (f32[12,128,128]{2,1,0:T(8,128)}, f32[12,128,128]{2,1,0:T(8,128)S(1)}, u32[]{:S(2)}) copy-start(f32[12,128,128]{2,1,0:T(8,128)S(1)} %fusion.19) | copy-start | bytes 2359300
  42.8 7.3 %copy-start.12 = (bf16[1,256,1536]{2,1,0:T(8,128)(2,1)S(1)}, bf16[1,256,1536]{2,1,0:T(8,128)(2,1)}, u32[]{:S(2)}) copy-start(bf16[1,256,1536]{2,1,0:T(8,128)(2,1)} %param.5) | copy-start | bytes 2359300
  44.2 25.7 %all-to-all-start.1 = ((f32[32,48,128]{2,1,0:T(8,128)}), f32[32,48,128]{2,1,0:T(8,128)}, u32[]{:S(2)}, u32[]{:S(2)}) async-start(f32[32,48,128]{2,1,0:T(8,128)} %copy.88), calls=%async_computation.1 | async-start | bytes 1572864 | tf_op jit(solution)/shard_map/all_to_all | solution.py:28
  50.1 152.2 %all-gather.3.cloned.1.call-start = ((), (), s32[]{:S(2)}) async-start(), calls=%async_computation.4 | async-start | bytes 16842752 | tf_op jit(solution)/shard_map/all_gather | solution.py:77
  51.8 20.4 %copy-start.4 = (bf16[1,256,1536]{1,2,0:T(8,128)(2,1)}, bf16[1,256,1536]{1,2,0:T(8,128)(2,1)S(1)}, u32[]{:S(2)}) copy-start(bf16[1,256,1536]{1,2,0:T(8,128)(2,1)S(1)} %copy.94) | copy-start | bytes 2359300
  51.9 0.8 copy-start.13
  52.7 1.2 copy-start.1
  69.9 1.9 copy-start.10
  71.7 1.6 copy-start.14
  72.2 1.1 copy-start
  78.1 27.8 %copy-start.5 = (f32[12,128,128]{1,2,0:T(8,128)}, f32[12,128,128]{1,2,0:T(8,128)S(1)}, u32[]{:S(2)}) copy-start(f32[12,128,128]{1,2,0:T(8,128)S(1)} %fusion.22) | copy-start | bytes 2359300
  107.2 27.0 %all-to-all-start.3 = ((f32[32,48,128]{2,1,0:T(8,128)}), f32[32,48,128]{2,1,0:T(8,128)}, u32[]{:S(2)}, u32[]{:S(2)}) async-start(f32[32,48,128]{2,1,0:T(8,128)} %copy.100), calls=%async_computation.3 | async-start | bytes 1572864 | tf_op jit(solution)/shard_map/all_to_all | solution.py:28
  115.6 1.2 copy-start.2
  122.6 3.1 %copy-start.3 = (bf16[12,256,256]{2,1,0:T(8,128)(2,1)S(1)}, bf16[12,256,256]{2,1,0:T(8,128)(2,1)}, u32[]{:S(2)}) copy-start(bf16[12,256,256]{2,1,0:T(8,128)(2,1)} %copy-done.2) | copy-start | bytes 4718596
  125.6 8.6 %copy-start.6 = (f32[12,128,128]{1,2,0:T(8,128)S(1)}, f32[12,128,128]{1,2,0:T(8,128)}, u32[]{:S(2)}) copy-start(f32[12,128,128]{1,2,0:T(8,128)} %copy-done.5) | copy-start | bytes 2359300
  134.2 1.6 copy-start.9
  136.3 1.7 copy-start.8
Sparse Core Ops, SparseCore 0:
  74.9 127.3 all-gather.2
